TPU v7x, 256 devices: a whole 4x4x8 slice. The times are simulated.
256 devices in a mesh: lat: 16 (over z_lo, x, core), lon: 4 (over y), bin: 4 (over z_hi).
Axes of the slice: x: 4, y: 4, z: 8 (z_hi: 4, z_lo: 2; z = z_hi * 2 + z_lo), core: 2. Of those that a mesh axis runs over, the one named last changes fastest.
Arguments:
- inputs: bfloat16 [512, 1024, 128], P(('lat', 'bin'), 'lon'), may hold values from -70 to 70
- conv_one: bfloat16 [3, 3, 128, 128], replicated, may hold values from -0.1875 to 0.1875
- conv_two: bfloat16 [3, 3, 128, 128], replicated, may hold values from -0.1875 to 0.1875
- head_weight: bfloat16 [4, 128, 512], P(None, None, 'bin'), may hold values from -45.078057 to 45.078057
- targets: int32 [4, 512, 1024], P(None, 'lat', 'lon'), may hold values from 0 to 511
Outputs:
- loss_mean: float32 [], replicated
- grad_conv_one: float32 [3, 3, 128, 128], replicated
- grad_conv_two: float32 [3, 3, 128, 128], replicated
- grad_heads: float32 [4, 128, 512], P(None, None, 'bin')
All inputs are finite; a program needn't handle non-finite values.
Results may differ from a plain program's by a relative error of at most 0.0035.
The roundings to bfloat16 on the way count: a program that leaves them out, or rounds other values in their place, can miss the bound.
Values may be sent and summed in bfloat16 or wider, within the bound.
A program may use at most 64 MiB of HBM per device.

v0:
```python
import math
import jax
import jax.numpy as jnp
from jax import lax
from jax.sharding import PartitionSpec as P


def extended(shard, sides, width):
    for axis, dim in sides:
        devices, length = (lax.axis_size(axis), shard.shape[dim])
        up = [(i, (i + 1) % devices) for i in range(devices - 1)]
        down = [(j, i) for i, j in up]
        last = lax.slice_in_dim(shard, length - width, length, axis=dim)
        leading = lax.slice_in_dim(shard, 0, width, axis=dim)
        before = lax.ppermute(last, axis, up)
        after = lax.ppermute(leading, axis, down)
        shard = jnp.concatenate([before, shard, after], axis=dim)
    return shard


def merged(shard, axis, combine):
    everything = jax.tree.map(lambda part: lax.all_gather(part, axis), shard)
    leading = jax.tree.map(lambda part: part[0], everything)

    def lap(k, so_far):
        return combine(so_far, jax.tree.map(lambda part: part[k], everything))

    return lax.fori_loop(1, lax.axis_size(axis), lap, leading)


def patches(padded, grid_rows, grid_cols):
    slices = [padded[a : a + grid_rows, b : b + grid_cols] for a in range(3) for b in range(3)]
    return jnp.concatenate(slices, axis=2).reshape(grid_rows * grid_cols, -1)


def rimmed(values_in):
    return extended(values_in, ((("lat", "bin"), 0), ("lon", 1)), 1)


def softmax_join(left, right):
    highest = jnp.maximum(left[0], right[0])
    summed = left[1] * jnp.exp(left[0] - highest) + right[1] * jnp.exp(right[0] - highest)
    return (highest, summed, left[2] + right[2])


def per_device(inputs, conv_one, conv_two, head_weight, targets):
    grid_rows, grid_cols, channels = inputs.shape
    head_count = head_weight.shape[0]
    cells_all = (
        grid_rows * lax.axis_size("lat") * lax.axis_size("bin") * grid_cols * lax.axis_size("lon")
    )
    loss_scale = 1.0 / math.sqrt(head_count * cells_all)
    inner_one = patches(rimmed(inputs), grid_rows, grid_cols)
    pre_one = jnp.dot(
        inner_one, conv_one.reshape(9 * channels, channels), preferred_element_type=jnp.float32
    )
    act_one = jnp.maximum(pre_one, 0.0).astype(jnp.bfloat16)
    inner_two = patches(
        rimmed(act_one.reshape(grid_rows, grid_cols, channels)), grid_rows, grid_cols
    )
    pre_two = jnp.dot(
        inner_two, conv_two.reshape(9 * channels, channels), preferred_element_type=jnp.float32
    )
    act_two = jnp.maximum(pre_two, 0.0).astype(jnp.bfloat16)
    gathered = lax.all_gather(
        act_two.reshape(grid_rows, grid_cols, channels), "bin", axis=0, tiled=True
    )
    features = gathered.reshape(-1, channels)
    labels = targets.reshape(head_count, -1)
    first_bin = lax.axis_index("bin") * head_weight.shape[2]
    cell_count = features.shape[0]
    bin_width = head_weight.shape[2]
    block_rows = math.gcd(cell_count, 1024)
    block_count = cell_count // block_rows
    feat_blocks = features.reshape(block_count, block_rows, channels)
    label_blocks = labels.reshape(head_count, block_count, block_rows).transpose(1, 0, 2)
    columns = jnp.arange(bin_width, dtype=jnp.int32)[None, :] + first_bin

    def head_stats(inputs_now):
        feat_rows, label_rows = inputs_now
        maxima, totals, picked = ([], [], [])
        for k in range(head_count):
            logits = jnp.dot(feat_rows, head_weight[k], preferred_element_type=jnp.float32)
            highest = jnp.max(logits, axis=1)
            maxima.append(highest)
            totals.append(jnp.sum(jnp.exp(logits - highest[:, None]), axis=1))
            picked.append(
                jnp.sum(jnp.where(columns == label_rows[k][:, None], logits, 0.0), axis=1)
            )
        return (jnp.stack(maxima), jnp.stack(totals), jnp.stack(picked))

    maxima, totals, picked = lax.map(head_stats, (feat_blocks, label_blocks))
    maxima, totals, picked = merged((maxima, totals, picked), "bin", softmax_join)
    log_total = maxima + jnp.log(totals)
    loss_part = jnp.sum(log_total - picked)

    def backward(gradients, inputs_now):
        feat_rows, label_rows, total_rows = inputs_now
        hidden_back = jnp.zeros((block_rows, channels), jnp.float32)
        for k in range(head_count):
            logits = jnp.dot(feat_rows, head_weight[k], preferred_element_type=jnp.float32)
            chosen = columns == label_rows[k][:, None]
            logit_grad = (
                (jnp.exp(logits - total_rows[k][:, None]) - jnp.where(chosen, 1.0, 0.0))
                * loss_scale
            ).astype(jnp.bfloat16)
            gradients = gradients.at[k].add(
                jnp.einsum("nc,nv->cv", feat_rows, logit_grad, preferred_element_type=jnp.float32)
            )
            hidden_back = hidden_back + jnp.einsum(
                "nv,cv->nc", logit_grad, head_weight[k], preferred_element_type=jnp.float32
            )
        return (gradients, hidden_back)

    start = jnp.zeros((head_count, channels, bin_width), jnp.float32)
    head_grads, backs = lax.scan(backward, start, (feat_blocks, label_blocks, log_total))
    hidden_back = backs.reshape(cell_count, channels)
    hidden_back = lax.psum_scatter(hidden_back, "bin", scatter_dimension=0, tiled=True)
    back_two = jnp.where(pre_two > 0, hidden_back, 0.0).astype(jnp.bfloat16)
    grad_two = jnp.einsum("nk,nc->kc", inner_two, back_two, preferred_element_type=jnp.float32)
    flipped = conv_two[::-1, ::-1].transpose(0, 1, 3, 2).reshape(9 * channels, channels)
    outer_two = patches(
        rimmed(back_two.reshape(grid_rows, grid_cols, channels)), grid_rows, grid_cols
    )
    back_act = jnp.dot(outer_two, flipped, preferred_element_type=jnp.float32)
    back_one = jnp.where(pre_one > 0, back_act, 0.0).astype(jnp.bfloat16)
    grad_one = jnp.einsum("nk,nc->kc", inner_one, back_one, preferred_element_type=jnp.float32)
    grad_one, grad_two = lax.psum((grad_one, grad_two), ("lat", "lon", "bin"))
    head_grads, loss_sum = lax.psum((head_grads, loss_part), ("lat", "lon"))
    loss_mean = loss_sum / (head_count * cells_all)
    grad_conv_one = grad_one.reshape(3, 3, channels, channels)
    grad_conv_two = grad_two.reshape(3, 3, channels, channels)
    return (loss_mean, grad_conv_one, grad_conv_two, head_grads)


def solution(mesh):
    in_specs = (
        P(("lat", "bin"), "lon", None),
        P(),
        P(),
        P(None, None, "bin"),
        P(None, "lat", "lon"),
    )
    out_specs = (P(), P(), P(), P(None, None, "bin"))
    return jax.shard_map(
        per_device, mesh=mesh, in_specs=in_specs, out_specs=out_specs, check_vma=False
    )
```

profile of v0, /device:TPU:8, one launch (start us, length us, event | category | flops | bytes accessed | tf_op | source)
XLA Modules:
  0.0 1140.5 jit_solution(2076384683649284297)
XLA Ops:
  8.2 5.2 collective-permute-start
  16.4 6.6 collective-permute-done.1
  23.0 3.5 collective-permute-start.2
  26.5 2.4 collective-permute-start.3
  33.4 2.4 maximum_convert_fusion.1
  37.2 6.5 collective-permute-start.4
  47.9 3.5 collective-permute-start.6
  57.8 2.5 maximum_convert_fusion
  60.6 55.4 %all-gather.5.cloned.1.call-done = bf16[32,256,128]{2,1,0:T(8,128)(2,1)} async-done(((bf16[8,256,128]{2,1,0:T(8,128)(2,1)}), bf16[32,256,128]{2,1,0:T(8,128)(2,1)}) %all-gather.5.cloned.1.call-update) | async-done | bytes 2097168 | tf_op jit(solution)/shard_map/all_gather | solution.py:65
  115.9 54.6 %while.55 = (s32[]{:T(128)}, f32[8,4,1024]{2,1,0:T(4,128)S(1)}, f32[8,4,1024]{2,1,0:T(4,128)}, f32[8,4,1024]{2,1,0:T(4,128)}, bf16[8,1024,128]{2,1,0:T(8,128)(2,...) while((s32[]{:T(128)}, f32[8,4,1024]{2,1,0:T(4,128)S(1)}, ...), condition=%wide.region_13.14_spmd.clone, body=%wide.region_0.13_spmd.clone.sunk | while | flops 137388160 | bytes 5588181 | solution.py:92
  171.2 16.7 %all-gather = f32[32,4,1024]{2,1,0:T(4,128)S(1)} all-gather(f32[8,4,1024]{2,1,0:T(4,128)S(1)} %get-tuple-element.411), channel_id=2, replica_groups=mesh['lat'=16,'lon'=4,'bin'=4] {'bin'}, dimensions={0}, use_global_device_ids=true | all-gather | bytes 655360 | tf_op jit(solution)/shard_map/all_gather | solution.py:22
  187.8 16.7 %all-gather.1 = f32[32,4,1024]{2,1,0:T(4,128)S(1)} all-gather(f32[8,4,1024]{2,1,0:T(4,128)} %get-tuple-element.412), channel_id=3, replica_groups=mesh['lat'=16,'lon'=4,'bin'=4] {'bin'}, dimensions={0}, use_global_device_ids=true | all-gather | bytes 655360 | tf_op jit(solution)/shard_map/all_gather | solution.py:22
  204.5 16.5 %all-gather.2 = f32[32,4,1024]{2,1,0:T(4,128)S(1)} all-gather(f32[8,4,1024]{2,1,0:T(4,128)} %get-tuple-element.413), channel_id=4, replica_groups=mesh['lat'=16,'lon'=4,'bin'=4] {'bin'}, dimensions={0}, use_global_device_ids=true | all-gather | bytes 655360 | tf_op jit(solution)/shard_map/all_gather | solution.py:22
  221.8 3.5 while.54
  226.0 42.4 %while.56 = (s32[]{:T(128)}, f32[4,128,128]{2,1,0:T(8,128)S(1)}, f32[8,1024,128]{2,1,0:T(8,128)}, bf16[8,1024,128]{2,1,0:T(8,128)(2,1)S(1)}, bf16[4,128,128]{2,1...) while((s32[]{:T(128)}, f32[4,128,128]{2,1,0:T(8,128)S(1)}, ...), condition=%wide.region_19.20_spmd.clone, body=%wide.region_18.19_spmd.clone.sunk | while | flops 406257792 | bytes 9800433 | solution.py:116
  269.3 82.1 %reduce-scatter.2.cloned.1.call-done = f32[2048,128]{1,0:T(8,128)} async-done(((f32[8192,128]{1,0:T(8,128)}), f32[2048,128]{1,0:T(8,128)}) %reduce-scatter.2.cloned.1.call-update) | async-done | bytes 1048592 | tf_op jit(solution)/shard_map/reduce_scatter | solution.py:118
  354.1 5.4 collective-permute-start.8
  359.5 4.6 fusion.126
  364.1 2.4 collective-permute-start.11
  366.6 3.4 collective-permute-start.10
  376.4 8.8 fusion.101
  385.2 139.1 %psum.28 = f32[]{:T(128)} all-reduce(f32[]{:T(128)} %get-tuple-element.553), channel_id=1, replica_groups=mesh['lat'=16,'lon'=4,'bin'=4] {'lat','lon'}, use_global_device_ids=true, to_apply=%region_17.18 | all-reduce | flops 1 | bytes 8 | tf_op jit(solution)/shard_map/psum | solution.py:129
  525.0 335.9 %all-reduce.4.cloned.1.call-done = f32[4,128,128]{2,1,0:T(8,128)} async-done(((f32[4,128,128]{2,1,0:T(8,128)}), f32[4,128,128]{2,1,0:T(8,128)}) %all-reduce.4.cloned.1.call-update) | async-done | bytes 262160 | tf_op jit(solution)/shard_map/psum | solution.py:129
  860.9 266.5 %all-reduce.6.cloned.1.call-done = (f32[3,3,128,128]{3,2,1,0:T(8,128)}, f32[3,3,128,128]{3,2,1,0:T(8,128)}) async-done(((f32[3,3,128,128]{3,2,1,0:T(8,128)}, f32[3,3,128,128]{3,2,1,0:T(8,128)}), (f32[3,3,128,128]{3,2,1,0:T(8,128)}, f32[3,3,128,128]{3,2,1,0:T(8,128)})) %all-reduce.6.cloned.1.call-update) | async-done | bytes 1179664 | tf_op jit(solution)/shard_map/psum | solution.py:128
  (310 shorter events, 137.1 us)
Async XLA Ops:
  7.2 26.2 %copy-start = (bf16[3,3,128,128]{3,2,1,0:T(8,128)(2,1)S(1)}, bf16[3,3,128,128]{3,2,1,0:T(8,128)(2,1)}, u32[]{:S(2)}) copy-start(bf16[3,3,128,128]{3,2,1,0:T(8,128)(2,1)} %param.20) | copy-start | bytes 884740
  7.2 25.3 %copy-start.5 = (bf16[8,256,128]{2,1,0:T(8,128)(2,1)S(1)}, bf16[8,256,128]{2,1,0:T(8,128)(2,1)}, u32[]{:S(2)}) copy-start(bf16[8,256,128]{2,1,0:T(8,128)(2,1)} %param.19) | copy-start | bytes 1572868
  7.2 108.7 %all-gather.5.cloned.1.call-start = ((), (), s32[]{:S(2)}) async-start(), calls=%async_computation.1 | async-start | bytes 2621440 | tf_op jit(solution)/shard_map/all_gather | solution.py:65
  8.2 7.1 collective-permute-start
  13.4 9.6 collective-permute-start.1
  23.0 5.9 collective-permute-start.2
  26.5 5.5 collective-permute-start.3
  33.4 18.1 %copy-start.6 = (bf16[8,256,1152]{2,1,0:T(8,128)(2,1)}, bf16[8,256,1152]{2,1,0:T(8,128)(2,1)S(1)}, u32[]{:S(2)}) copy-start(bf16[8,256,1152]{2,1,0:T(8,128)(2,1)S(1)} %fusion.110) | copy-start | bytes 14155780
  35.9 8.8 collective-permute-start.5
  37.2 8.4 collective-permute-start.4
  45.6 6.0 collective-permute-start.7
  47.9 5.5 collective-permute-start.6
  55.4 60.5 %copy-start.3 = (bf16[4,128,128]{2,1,0:T(8,128)(2,1)S(1)}, bf16[4,128,128]{2,1,0:T(8,128)(2,1)}, u32[]{:S(2)}) copy-start(bf16[4,128,128]{2,1,0:T(8,128)(2,1)} %param.22) | copy-start | bytes 393220
  60.3 291.1 %reduce-scatter.2.cloned.1.call-start = ((), (), s32[]{:S(2)}) async-start(), calls=%async_computation.2 | async-start | bytes 5242880 | tf_op jit(solution)/shard_map/reduce_scatter | solution.py:118
  171.2 54.8 %copy-start.1 = (bf16[8,1024,128]{2,1,0:T(8,128)(2,1)S(1)}, bf16[8,1024,128]{2,1,0:T(8,128)(2,1)}, u32[]{:S(2)}) copy-start(bf16[8,1024,128]{2,1,0:T(8,128)(2,1)} %get-tuple-element.944) | copy-start | bytes 6291460
  204.5 16.5 %copy-start.8 = (f32[32,4,1024]{2,1,0:T(4,128)}, f32[32,4,1024]{2,1,0:T(4,128)S(1)}, u32[]{:S(2)}) copy-start(f32[32,4,1024]{2,1,0:T(4,128)S(1)} %all-gather.1) | copy-start | bytes 1572868
  226.0 42.5 %copy-start.12 = (bf16[3,3,128,128]{3,2,1,0:T(8,128)(2,1)S(1)}, bf16[3,3,128,128]{3,2,1,0:T(8,128)(2,1)}, u32[]{:S(2)}) copy-start(bf16[3,3,128,128]{3,2,1,0:T(8,128)(2,1)} %param.21) | copy-start | bytes 884740
  268.5 82.9 %copy-start.7 = (f32[2048,128]{1,0:T(8,128)S(1)}, f32[2048,128]{1,0:T(8,128)}, u32[]{:S(2)}) copy-start(f32[2048,128]{1,0:T(8,128)} %get-tuple-element.613) | copy-start | bytes 3145732
  268.5 592.4 %all-reduce.4.cloned.1.call-start = ((), (), s32[]{:S(2)}) async-start(), calls=%async_computation.3 | async-start | bytes 524288 | tf_op jit(solution)/shard_map/psum | solution.py:129
  269.2 858.1 %all-reduce.6.cloned.1.call-start = ((), (), s32[]{:S(2)}) async-start(), calls=%async_computation.4 | async-start | bytes 2359296 | tf_op jit(solution)/shard_map/psum | solution.py:128
  352.8 11.3 collective-permute-start.9
  354.1 10.0 collective-permute-start.8
  364.1 5.9 collective-permute-start.11
  366.6 5.5 collective-permute-start.10
  (8 other events, 18.2 us)
Sparse Core Ops, SparseCore 0:
  60.4 55.4 all-gather.4
  268.6 82.7 reduce-scatter.1
  354.8 506.0 all-reduce.3
  866.8 260.5 all-reduce.5
where the time goes:
time: 1140 us
  waiting for transfers between devices  755 us (66%)
  blocking collectives  189 us (17%)
  matrix products  92 us (8%)
  starting transfers between devices  38.7 us (3%)
  local copies, waits for them, and re-layouts  25.3 us (2%)
  other arithmetic  23.5 us (2%)
  between operations  16.2 us (1%)
    psum x1, waiting for transfers between devices, per_device(): head_grads, loss_sum = lax.psum((head_grads, loss_part), ('lat', 'lon'))  336 us
    psum x1, waiting for transfers between devices, per_device(): grad_one, grad_two = lax.psum((grad_one, grad_two), ('lat', 'lon', 'bin'))  267 us
    psum x1, blocking collectives, per_device(): head_grads, loss_sum = lax.psum((head_grads, loss_part), ('lat', 'lon'))  139 us
    reduce_scatter x1, waiting for transfers between devices, per_device(): lax.psum_scatter(hidden_back, 'bin', scatter_dimension=0, tiled=True)  82.1 us
    all_gather x1, waiting for transfers between devices, per_device(): lax.all_gather(act_two.reshape(grid_rows, grid_cols, channels), 'bin', ax...  55.4 us
    all_gather x3, blocking collectives, merged(): everything = jax.tree.map(lambda part: lax.all_gather(part, axis), shard)  49.9 us
    dot_general x32, matrix products, head_stats(): jnp.dot(feat_rows, head_weight[k], preferred_element_type=jnp.float32)  39.3 us
    ppermute x6, starting transfers between devices, extended(): before = lax.ppermute(last, axis, up)  27.5 us
  transfers between devices with their start and end apart: 16, of which 11 were waited for; matrix products, arithmetic and copies ran while one was open for 2% of the time, Pallas kernels for 0%

commit v1 on v0

--- a/solution.py
+++ b/solution.py
@@ -1,8 +1,17 @@
+import functools
 import math
 import jax
 import jax.numpy as jnp
 from jax import lax
 from jax.sharding import PartitionSpec as P
+from jax.lax import psum
+
+
+def open_the_group(inner_x, net_axis, mesh_ax):
+    return psum(psum(inner_x, axis_name=net_axis), mesh_ax)
+
+
+plan_pairs_all_here = functools.partial(open_the_group, net_axis=("lon", "bin"), mesh_ax="lat")
 
 
 def extended(shard, sides, width):
@@ -125,7 +134,7 @@
     back_act = jnp.dot(outer_two, flipped, preferred_element_type=jnp.float32)
     back_one = jnp.where(pre_one > 0, back_act, 0.0).astype(jnp.bfloat16)
     grad_one = jnp.einsum("nk,nc->kc", inner_one, back_one, preferred_element_type=jnp.float32)
-    grad_one, grad_two = lax.psum((grad_one, grad_two), ("lat", "lon", "bin"))
+    grad_one, grad_two = plan_pairs_all_here((grad_one, grad_two))
     head_grads, loss_sum = lax.psum((head_grads, loss_part), ("lat", "lon"))
     loss_mean = loss_sum / (head_count * cells_all)
     grad_conv_one = grad_one.reshape(3, 3, channels, channels)

time: 1140 us -> 1210 us (1.061)
  waiting for transfers between devices: 755 us -> 819 us
    psum x1, waiting for transfers between devices: 336 us -> 368 us  [per_device(): head_grads, loss_sum = lax.psum((head_grads, loss_part), ('lat', 'lon'))]
    psum x1 -> x2, waiting for transfers between devices: 267 us -> 297 us  [open_the_group(): return psum(psum(inner_x, axis_name=net_axis), mesh_ax)]
  transfers between devices with their start and end apart: 16 -> 17, of which waited for: 11 -> 12; matrix products, arithmetic and copies ran while one was open for 2% -> 1% of each run, Pallas kernels for 0% -> 0%
where the time goes in v1:
time: 1210 us
  waiting for transfers between devices  819 us (68%)
  blocking collectives  194 us (16%)
  matrix products  92.1 us (8%)
  starting transfers between devices  38.7 us (3%)
  local copies, waits for them, and re-layouts  24.9 us (2%)
  other arithmetic  23.5 us (2%)
  between operations  16.2 us (1%)
    psum x1, waiting for transfers between devices, per_device(): head_grads, loss_sum = lax.psum((head_grads, loss_part), ('lat', 'lon'))  368 us
    psum x2, waiting for transfers between devices, open_the_group(): return psum(psum(inner_x, axis_name=net_axis), mesh_ax)  297 us
    psum x1, blocking collectives, per_device(): head_grads, loss_sum = lax.psum((head_grads, loss_part), ('lat', 'lon'))  144 us
    reduce_scatter x1, waiting for transfers between devices, per_device(): lax.psum_scatter(hidden_back, 'bin', scatter_dimension=0, tiled=True)  83.2 us
    all_gather x1, waiting for transfers between devices, per_device(): lax.all_gather(act_two.reshape(grid_rows, grid_cols, channels), 'bin', ax...  55.4 us
    all_gather x3, blocking collectives, merged(): everything = jax.tree.map(lambda part: lax.all_gather(part, axis), shard)  49.3 us
    dot_general x32, matrix products, head_stats(): jnp.dot(feat_rows, head_weight[k], preferred_element_type=jnp.float32)  39.3 us
    ppermute x6, starting transfers between devices, extended(): before = lax.ppermute(last, axis, up)  27.5 us
  transfers between devices with their start and end apart: 17, of which 12 were waited for; matrix products, arithmetic and copies ran while one was open for 1% of the time, Pallas kernels for 0%

profile of v1, /device:TPU:8, one launch (start us, length us, event | category | flops | bytes accessed | tf_op | source)
XLA Modules:
  0.0 1208.9 jit_solution(14192364226053998317)
XLA Ops:
  8.2 5.2 collective-permute-start
  16.4 6.6 collective-permute-done.1
  23.0 3.5 collective-permute-start.2
  33.4 2.5 maximum_convert_fusion.1
  37.2 6.5 collective-permute-start.4
  47.9 3.5 collective-permute-start.6
  57.8 2.5 maximum_convert_fusion
  60.6 55.4 %all-gather.5.cloned.1.call-done = bf16[32,256,128]{2,1,0:T(8,128)(2,1)} async-done(((bf16[8,256,128]{2,1,0:T(8,128)(2,1)}), bf16[32,256,128]{2,1,0:T(8,128)(2,1)}) %all-gather.5.cloned.1.call-update) | async-done | bytes 2097168 | tf_op jit(solution)/shard_map/all_gather | solution.py:74
  115.9 54.6 %while.55 = (s32[]{:T(128)}, f32[8,4,1024]{2,1,0:T(4,128)S(1)}, f32[8,4,1024]{2,1,0:T(4,128)}, f32[8,4,1024]{2,1,0:T(4,128)}, bf16[8,1024,128]{2,1,0:T(8,128)(2,...) while((s32[]{:T(128)}, f32[8,4,1024]{2,1,0:T(4,128)S(1)}, ...), condition=%wide.region_13.14_spmd.clone, body=%wide.region_0.13_spmd.clone.sunk | while | flops 137388160 | bytes 5588181 | solution.py:101
  171.2 16.7 %all-gather = f32[32,4,1024]{2,1,0:T(4,128)S(1)} all-gather(f32[8,4,1024]{2,1,0:T(4,128)S(1)} %get-tuple-element.411), channel_id=2, replica_groups=mesh['lat'=16,'lon'=4,'bin'=4] {'bin'}, dimensions={0}, use_global_device_ids=true | all-gather | bytes 655360 | tf_op jit(solution)/shard_map/all_gather | solution.py:31
  187.8 16.8 %all-gather.1 = f32[32,4,1024]{2,1,0:T(4,128)S(1)} all-gather(f32[8,4,1024]{2,1,0:T(4,128)} %get-tuple-element.412), channel_id=3, replica_groups=mesh['lat'=16,'lon'=4,'bin'=4] {'bin'}, dimensions={0}, use_global_device_ids=true | all-gather | bytes 655360 | tf_op jit(solution)/shard_map/all_gather | solution.py:31
  204.7 15.9 %all-gather.2 = f32[32,4,1024]{2,1,0:T(4,128)S(1)} all-gather(f32[8,4,1024]{2,1,0:T(4,128)} %get-tuple-element.413), channel_id=4, replica_groups=mesh['lat'=16,'lon'=4,'bin'=4] {'bin'}, dimensions={0}, use_global_device_ids=true | all-gather | bytes 655360 | tf_op jit(solution)/shard_map/all_gather | solution.py:31
  221.3 3.5 while.54
  225.5 42.5 %while.56 = (s32[]{:T(128)}, f32[4,128,128]{2,1,0:T(8,128)S(1)}, f32[8,1024,128]{2,1,0:T(8,128)}, bf16[8,1024,128]{2,1,0:T(8,128)(2,1)S(1)}, bf16[4,128,128]{2,1...) while((s32[]{:T(128)}, f32[4,128,128]{2,1,0:T(8,128)S(1)}, ...), condition=%wide.region_19.20_spmd.clone, body=%wide.region_18.19_spmd.clone.sunk | while | flops 406257792 | bytes 9800433 | solution.py:125
  268.3 83.2 %reduce-scatter.2.cloned.1.call-done = f32[2048,128]{1,0:T(8,128)} async-done(((f32[8192,128]{1,0:T(8,128)}), f32[2048,128]{1,0:T(8,128)}) %reduce-scatter.2.cloned.1.call-update) | async-done | bytes 1048592 | tf_op jit(solution)/shard_map/reduce_scatter | solution.py:127
  354.2 5.4 collective-permute-start.8
  359.6 4.6 fusion.126
  364.3 2.4 collective-permute-start.11
  366.7 3.5 collective-permute-start.10
  376.5 8.8 fusion.101
  385.9 167.7 %all-reduce.8.cloned.1.call-done = (f32[1152,128]{1,0:T(8,128)}, f32[1152,128]{1,0:T(8,128)}) async-done(((f32[1152,128]{1,0:T(8,128)}, f32[1152,128]{1,0:T(8,128)}), (f32[1152,128]{1,0:T(8,128)}, f32[1152,128]{1,0:T(8,128)})) %all-reduce.8.cloned.1.call-update) | async-done | bytes 1179664 | tf_op jit(solution)/shard_map/psum | solution.py:11
  553.7 144.3 %psum.42 = f32[]{:T(128)} all-reduce(f32[]{:T(128)} %get-tuple-element.555), channel_id=1, replica_groups=mesh['lat'=16,'lon'=4,'bin'=4] {'lat','lon'}, use_global_device_ids=true, to_apply=%region_17.18 | all-reduce | flops 1 | bytes 8 | tf_op jit(solution)/shard_map/psum | solution.py:138
  698.7 367.8 %all-reduce.6.cloned.1.call-done = f32[4,128,128]{2,1,0:T(8,128)} async-done(((f32[4,128,128]{2,1,0:T(8,128)}), f32[4,128,128]{2,1,0:T(8,128)}) %all-reduce.6.cloned.1.call-update) | async-done | bytes 262160 | tf_op jit(solution)/shard_map/psum | solution.py:138
  1066.5 129.2 %all-reduce.10.cloned.1.call-done = (f32[3,3,128,128]{3,2,1,0:T(8,128)}, f32[3,3,128,128]{3,2,1,0:T(8,128)}) async-done(((f32[3,3,128,128]{3,2,1,0:T(8,128)}, f32[3,3,128,128]{3,2,1,0:T(8,128)}), (f32[3,3,128,128]{3,2,1,0:T(8,128)}, f32[3,3,128,128]{3,2,1,0:T(8,128)})) %all-reduce.10.cloned.1.call-update) | async-done | bytes 1179664 | tf_op jit(solution)/shard_map/psum | solution.py:11
  (313 shorter events, 139.7 us)
Async XLA Ops:
  7.2 26.2 %copy-start = (bf16[3,3,128,128]{3,2,1,0:T(8,128)(2,1)S(1)}, bf16[3,3,128,128]{3,2,1,0:T(8,128)(2,1)}, u32[]{:S(2)}) copy-start(bf16[3,3,128,128]{3,2,1,0:T(8,128)(2,1)} %param.20) | copy-start | bytes 884740
  7.2 25.3 %copy-start.5 = (bf16[8,256,128]{2,1,0:T(8,128)(2,1)S(1)}, bf16[8,256,128]{2,1,0:T(8,128)(2,1)}, u32[]{:S(2)}) copy-start(bf16[8,256,128]{2,1,0:T(8,128)(2,1)} %param.19) | copy-start | bytes 1572868
  7.2 108.7 %all-gather.5.cloned.1.call-start = ((), (), s32[]{:S(2)}) async-start(), calls=%async_computation.1 | async-start | bytes 2621440 | tf_op jit(solution)/shard_map/all_gather | solution.py:74
  8.2 7.1 collective-permute-start
  13.4 9.6 collective-permute-start.1
  23.0 5.9 collective-permute-start.2
  26.5 5.5 collective-permute-start.3
  35.9 8.8 collective-permute-start.5
  37.2 8.4 collective-permute-start.4
  45.6 6.0 collective-permute-start.7
  47.9 5.5 collective-permute-start.6
  55.4 60.5 %copy-start.3 = (bf16[4,128,128]{2,1,0:T(8,128)(2,1)S(1)}, bf16[4,128,128]{2,1,0:T(8,128)(2,1)}, u32[]{:S(2)}) copy-start(bf16[4,128,128]{2,1,0:T(8,128)(2,1)} %param.22) | copy-start | bytes 393220
  60.3 291.2 %reduce-scatter.2.cloned.1.call-start = ((), (), s32[]{:S(2)}) async-start(), calls=%async_computation.2 | async-start | bytes 5242880 | tf_op jit(solution)/shard_map/reduce_scatter | solution.py:127
  171.2 54.3 %copy-start.1 = (bf16[8,1024,128]{2,1,0:T(8,128)(2,1)S(1)}, bf16[8,1024,128]{2,1,0:T(8,128)(2,1)}, u32[]{:S(2)}) copy-start(bf16[8,1024,128]{2,1,0:T(8,128)(2,1)} %get-tuple-element.950) | copy-start | bytes 6291460
  225.5 42.6 %copy-start.12 = (bf16[3,3,128,128]{3,2,1,0:T(8,128)(2,1)S(1)}, bf16[3,3,128,128]{3,2,1,0:T(8,128)(2,1)}, u32[]{:S(2)}) copy-start(bf16[3,3,128,128]{3,2,1,0:T(8,128)(2,1)} %param.21) | copy-start | bytes 884740
  268.0 96.2 %copy-start.4 = (f32[4,128,128]{2,1,0:T(8,128)}, f32[4,128,128]{2,1,0:T(8,128)S(1)}, u32[]{:S(2)}) copy-start(f32[4,128,128]{2,1,0:T(8,128)S(1)} %get-tuple-element.418) | copy-start | bytes 786436
  268.0 83.5 %copy-start.7 = (f32[2048,128]{1,0:T(8,128)S(1)}, f32[2048,128]{1,0:T(8,128)}, u32[]{:S(2)}) copy-start(f32[2048,128]{1,0:T(8,128)} %get-tuple-element.615) | copy-start | bytes 3145732
  268.0 285.6 %all-reduce.8.cloned.1.call-start = ((), (), s32[]{:S(2)}) async-start(), calls=%async_computation.4 | async-start | bytes 2359296 | tf_op jit(solution)/shard_map/psum | solution.py:11
  352.9 11.3 collective-permute-start.9
  354.2 10.1 collective-permute-start.8
  364.3 5.9 collective-permute-start.11
  366.7 5.5 collective-permute-start.10
  385.3 681.2 %all-reduce.6.cloned.1.call-start = ((), (), s32[]{:S(2)}) async-start(), calls=%async_computation.3 | async-start | bytes 524288 | tf_op jit(solution)/shard_map/psum | solution.py:138
  385.9 809.9 %all-reduce.10.cloned.1.call-start = ((), (), s32[]{:S(2)}) async-start(), calls=%async_computation.5 | async-start | bytes 2359296 | tf_op jit(solution)/shard_map/psum | solution.py:11
  (9 other events, 51.5 us)
Sparse Core Ops, SparseCore 0:
  60.4 55.4 all-gather.4
  268.2 83.3 reduce-scatter.1
  385.4 168.1 all-reduce.7
  556.9 509.5 all-reduce.5
  1069.0 126.6 all-reduce.9
